TPU v7x, 512 devices: a whole 4x4x16 slice. The times are simulated.
512 devices in a mesh: seq: 64 (over z, y), ch: 8 (over x, core).
Axes of the slice: x: 4, y: 4, z: 16, core: 2. Of those that a mesh axis runs over, the one named last changes fastest.
Arguments:
- normalized_layer_entry: bfloat16 [8192, 4096], P('seq', 'ch'), may hold values from -6 to 6
- short_outer_query: bfloat16 [8192, 4096], P('seq', 'ch'), may hold values from -6 to 6
- short_inner_key: bfloat16 [8192, 4096], P('seq', 'ch'), may hold values from -6 to 6
- short_frozen_value: bfloat16 [8192, 4096], P('seq', 'ch'), may hold values from -6 to 6
- medium_outer_query: bfloat16 [8192, 4096], P('seq', 'ch'), may hold values from -6 to 6
- medium_inner_key: bfloat16 [8192, 4096], P('seq', 'ch'), may hold values from -6 to 6
- cotangent: bfloat16 [8192, 4096], P('seq', 'ch'), may hold values from -6 to 6
- adapter_down_factor: bfloat16 [64, 32, 4096], P('seq', None, 'ch'), may hold values from -0.09375 to 0.09375
- adapter_up_factor: bfloat16 [64, 32, 4096], P('seq', None, 'ch'), may hold values from -1 to 1
- token_clade: int32 [8192, 1], P('seq'), may hold values from 0 to 63; in each aligned block of 128 rows (0 to 127, 128 to 255, ...) at most 4 rows name the same one
- clade_storage_slot: int32 [64], replicated, may hold values from 0 to 63, each once
- short_group_filter: float32 [256, 7], P('ch'), may hold values from -2.4 to 2.4
- medium_undamped_filter: float32 [256, 128], P('ch'), may hold values from -0.6 to 0.6
- medium_decay_rate: float32 [256], P('ch'), may hold values from 0.003 to 0.06
Outputs:
- midrange_response: bfloat16 [8192, 4096], P('seq', 'ch')
- layer_entry_derivative: bfloat16 [8192, 4096], P('seq', 'ch')
- lowdim_projector_derivative: float32 [64, 32, 4096], P('seq', None, 'ch')
- lowdim_expander_derivative: float32 [64, 32, 4096], P('seq', None, 'ch')
- brief_convolution_derivative: float32 [256, 7], P('ch')
- midrange_raw_response_derivative: float32 [256, 128], P('ch')
Inputs may be any that keep to these rules, and one draw needn't show every extreme that they name: `token_clade`: among the 128 tokens of one device, no clade is named more than 4 times, a bound that some block reaches. `clade_storage_slot`: each slot holds exactly one clade's adapter.
All inputs are finite; a program needn't handle non-finite values.
Results may differ from a plain program's by a relative error of at most 0.012.
Values may be sent and summed in bfloat16 or wider, within the bound.
A program may use at most 64 MiB of HBM per device.

v0:
```python
import math
import jax
import jax.numpy as jnp
from jax import lax
from jax.sharding import PartitionSpec as P


def passed_along(value, axis, steps):
    count = lax.axis_size(axis)
    first, last = (max(0, -steps), min(count, count - steps))
    return lax.ppermute(value, axis, [(source, source + steps) for source in range(first, last)])


def band_matrix(kernel, out_len):
    groups, taps = kernel.shape
    full_len = out_len + taps - 1
    reversed_taps = kernel[:, ::-1]
    padded = jnp.concatenate(
        [reversed_taps, jnp.zeros((groups, full_len + 1 - taps), kernel.dtype)], axis=1
    )
    repeated_groups = jnp.tile(padded, (1, out_len))[:, : out_len * full_len]
    return repeated_groups.reshape(groups, out_len, full_len)


def causal_local(extended, kernel):
    groups, taps = kernel.shape
    full_len, feature_lanes = extended.shape
    out_len = full_len - taps + 1
    group_size = feature_lanes // groups
    per_block = math.gcd(groups, 8)
    blocks = groups // per_block
    shaped = extended.reshape(full_len, blocks, per_block, group_size).transpose(1, 2, 3, 0)
    kernel_blocks = kernel.reshape(blocks, per_block, taps)

    def one_block(pair):
        data, kern = pair
        band = band_matrix(kern, out_len)
        return jnp.einsum("gts,gcs->gct", band, data, precision=lax.Precision.HIGHEST)

    result = lax.map(one_block, (shaped, kernel_blocks))
    return result.transpose(3, 0, 1, 2).reshape(out_len, feature_lanes)


def to_slots(placing, values):
    return jnp.dot(placing, values, preferred_element_type=jnp.float32).astype(jnp.bfloat16)


def contract_last(left, right):
    return lax.dot_general(
        left, right, (((1,), (1,)), ((), ())), preferred_element_type=jnp.float32
    )


def contract_first(left, right):
    return lax.dot_general(
        left, right, (((0,), (0,)), ((), ())), preferred_element_type=jnp.float32
    )


def select_codes(products, owner_hot):
    sequence_length = products.shape[0]
    return jnp.sum(
        products.reshape(sequence_length, owner_hot.shape[1], -1) * owner_hot[:, :, None], axis=1
    )


def spread_codes(lineage_labels, owner_hot):
    sequence_length = lineage_labels.shape[0]
    return (
        (owner_hot[:, :, None] * lineage_labels.astype(jnp.float32)[:, None, :])
        .reshape(sequence_length, -1)
        .astype(jnp.bfloat16)
    )


def on_device(
    normalized_layer_entry,
    short_outer_query,
    short_inner_key,
    short_frozen_value,
    medium_outer_query,
    medium_inner_key,
    cotangent,
    adapter_down_factor,
    adapter_up_factor,
    token_clade,
    clade_storage_slot,
    short_group_filter,
    medium_undamped_filter,
    medium_decay_rate,
):
    sequence_length, feature_lanes = normalized_layer_entry.shape
    seq_count = lax.axis_size("seq")
    capacity = max(2, 2 * sequence_length // seq_count)
    slot_count = seq_count * capacity
    lowdim_breadth = adapter_down_factor.shape[1]
    short_len = short_group_filter.shape[1]
    medium_len = medium_undamped_filter.shape[1]
    group_size = feature_lanes // short_group_filter.shape[0]
    clade_hot = (
        token_clade[:, 0][:, None] == jnp.arange(seq_count, dtype=jnp.int32)[None, :]
    ).astype(jnp.float32)
    owner_token = jnp.sum(clade_hot * clade_storage_slot[None, :].astype(jnp.float32), axis=1)
    earlier_mask = (
        jnp.arange(sequence_length)[:, None] > jnp.arange(sequence_length)[None, :]
    ).astype(jnp.float32)
    earlier = jnp.dot(earlier_mask, clade_hot, precision=lax.Precision.HIGHEST)
    rank_inside = jnp.sum(clade_hot * earlier, axis=1)
    position = owner_token * capacity + rank_inside
    placing = (jnp.arange(slot_count, dtype=jnp.float32)[:, None] == position[None, :]).astype(
        jnp.bfloat16
    )
    owner_hot = (owner_token[:, None] == jnp.arange(seq_count, dtype=jnp.float32)[None, :]).astype(
        jnp.float32
    )
    all_down, all_up = (
        lax.all_gather(adapter_down_factor, "seq", axis=0, tiled=True),
        lax.all_gather(adapter_up_factor, "seq", axis=0, tiled=True),
    )
    flat_down = all_down.reshape(seq_count * lowdim_breadth, feature_lanes)
    flat_up = all_up.reshape(seq_count * lowdim_breadth, feature_lanes)
    lineage_labels = lax.psum(
        select_codes(contract_last(normalized_layer_entry, flat_down), owner_hot), "ch"
    ).astype(jnp.bfloat16)
    adapter_update = (
        0.5
        * jnp.dot(
            spread_codes(lineage_labels, owner_hot), flat_up, preferred_element_type=jnp.float32
        )
    ).astype(jnp.bfloat16)
    short_in = (
        short_inner_key.astype(jnp.float32)
        * (short_frozen_value.astype(jnp.float32) + adapter_update.astype(jnp.float32))
    ).astype(jnp.bfloat16)
    short_head = passed_along(short_in[sequence_length - (short_len - 1) :], "seq", 1)
    short_ext = jnp.concatenate([short_head, short_in], axis=0).astype(jnp.float32)
    taps_index = jnp.arange(medium_len, dtype=jnp.float32)
    decay_envelope = jnp.exp(-medium_decay_rate[:, None] * taps_index[None, :])
    medium_taps = medium_undamped_filter * decay_envelope
    short_conv, short_pull = jax.vjp(lambda kern: causal_local(short_ext, kern), short_group_filter)
    medium_operator_input = (
        medium_inner_key.astype(jnp.float32) * short_outer_query.astype(jnp.float32) * short_conv
    ).astype(jnp.bfloat16)
    medium_head = passed_along(
        medium_operator_input[sequence_length - (medium_len - 1) :], "seq", 1
    )
    medium_ext = jnp.concatenate([medium_head, medium_operator_input], axis=0).astype(jnp.float32)
    medium_conv, medium_pull = jax.vjp(lambda kern: causal_local(medium_ext, kern), medium_taps)
    midrange_response = (medium_outer_query.astype(jnp.float32) * medium_conv).astype(jnp.bfloat16)
    medium_gradient = (
        cotangent.astype(jnp.float32) * medium_outer_query.astype(jnp.float32)
    ).astype(jnp.bfloat16)
    (medium_tap_grad,) = medium_pull(medium_gradient.astype(jnp.float32))
    medium_next = passed_along(medium_gradient[: medium_len - 1], "seq", -1)
    medium_span = jnp.concatenate([medium_gradient, medium_next], axis=0).astype(jnp.float32)
    medium_in_grad = causal_local(medium_span[::-1], medium_taps)[::-1]
    short_grad = (
        medium_in_grad
        * medium_inner_key.astype(jnp.float32)
        * short_outer_query.astype(jnp.float32)
    ).astype(jnp.bfloat16)
    (short_tap_grad,) = short_pull(short_grad.astype(jnp.float32))
    short_next = passed_along(short_grad[: short_len - 1], "seq", -1)
    short_span = jnp.concatenate([short_grad, short_next], axis=0).astype(jnp.float32)
    short_in_grad = causal_local(short_span[::-1], short_group_filter)[::-1]
    short_total, medium_total = lax.psum((short_tap_grad, medium_tap_grad * decay_envelope), "seq")
    filter_gradient_scale = 1.0 / math.sqrt(sequence_length * seq_count * group_size)
    brief_convolution_derivative = short_total * filter_gradient_scale
    midrange_raw_response_derivative = medium_total * filter_gradient_scale
    correction_delta_derivative = (
        0.5 * short_in_grad * short_inner_key.astype(jnp.float32)
    ).astype(jnp.bfloat16)
    correction_multiplier = 1.0 / math.sqrt(sequence_length)
    lineage_labels_derivative = lax.psum(
        select_codes(contract_last(correction_delta_derivative, flat_up), owner_hot), "ch"
    ).astype(jnp.bfloat16)
    layer_entry_derivative = jnp.dot(
        spread_codes(lineage_labels_derivative, owner_hot),
        flat_down,
        preferred_element_type=jnp.float32,
    ).astype(jnp.bfloat16)
    packed = (
        to_slots(placing, normalized_layer_entry).reshape(seq_count, capacity, feature_lanes),
        to_slots(placing, lineage_labels).reshape(seq_count, capacity, lowdim_breadth),
        to_slots(placing, correction_delta_derivative).reshape(seq_count, capacity, feature_lanes),
        to_slots(placing, lineage_labels_derivative).reshape(seq_count, capacity, lowdim_breadth),
    )
    got_input, got_codes, got_delta, got_codes_grad = (
        lax.all_to_all(packed[0], "seq", split_axis=0, concat_axis=0, tiled=True),
        lax.all_to_all(packed[1], "seq", split_axis=0, concat_axis=0, tiled=True),
        lax.all_to_all(packed[2], "seq", split_axis=0, concat_axis=0, tiled=True),
        lax.all_to_all(packed[3], "seq", split_axis=0, concat_axis=0, tiled=True),
    )
    lowdim_expander_derivative = (
        contract_first(
            got_codes.reshape(slot_count, lowdim_breadth),
            got_delta.reshape(slot_count, feature_lanes),
        )
        * correction_multiplier
    )
    lowdim_projector_derivative = (
        contract_first(
            got_codes_grad.reshape(slot_count, lowdim_breadth),
            got_input.reshape(slot_count, feature_lanes),
        )
        * correction_multiplier
    )
    return (
        midrange_response,
        layer_entry_derivative,
        lowdim_projector_derivative.reshape(1, lowdim_breadth, feature_lanes),
        lowdim_expander_derivative.reshape(1, lowdim_breadth, feature_lanes),
        brief_convolution_derivative,
        midrange_raw_response_derivative,
    )


def solution(mesh):
    return jax.shard_map(
        on_device,
        mesh=mesh,
        in_specs=(
            P("seq", "ch"),
            P("seq", "ch"),
            P("seq", "ch"),
            P("seq", "ch"),
            P("seq", "ch"),
            P("seq", "ch"),
            P("seq", "ch"),
            P("seq", None, "ch"),
            P("seq", None, "ch"),
            P("seq", None),
            P(),
            P("ch", None),
            P("ch", None),
            P("ch"),
        ),
        out_specs=(
            P("seq", "ch"),
            P("seq", "ch"),
            P("seq", None, "ch"),
            P("seq", None, "ch"),
            P("ch", None),
            P("ch", None),
        ),
        check_vma=False,
    )
```

profile of v0, /device:TPU:2, one launch (start us, length us, event | category | flops | bytes accessed | tf_op | source)
XLA Modules:
  0.0 734.2 jit_solution(13968584702329256065)
XLA Ops:
  15.2 20.2 %all-to-all-start.1 = ((bf16[64,4,512]{2,1,0:T(4,128)(2,1)}), bf16[64,4,512]{2,1,0:T(4,128)(2,1)}, u32[]{:S(2)}, u32[]{:S(2)}) async-start(bf16[64,4,512]{2,1,0:T(4,128)(2,1)} %reshape.205), calls=%async_computation.1 | async-start | bytes 524288 | tf_op jit(solution)/shard_map/all_to_all | solution.py:189
  37.7 10.5 %while.70 = (s32[]{:T(128)}, f32[4,8,16,128]{3,2,1,0:T(8,128)S(1)}, f32[4,8,16,255]{3,2,1,0:T(8,128)S(1)}, f32[4,8,128]{2,1,0:T(8,128)S(1)}, s32[]{:T(128)}, /*index=5*/f32[]{:T(128)}) while((s32[]{:T(128)}, f32[4,8,16,128]{3,2,1,0:T(8,128)S(1)}, f32[4,8,16,255]{3,2,1,0:T(8,128)S(1)}, f32[4,8,128]{2,1,0:T(8,128)S(1)}, s32[]{:T(128)}, ...), condition=%wide.region_8.9_spmd, body=%wide.region_7.8_spmd.sunk | while | flops 50135040 | bytes 6509645 | solution.py:40
  51.8 3.2 collective-permute-done.3
  56.5 14.3 %while.71 = (s32[]{:T(128)}, f32[4,8,16,128]{3,2,1,0:T(8,128)}, f32[4,8,16,134]{3,2,1,0:T(8,128)S(1)}, f32[4,8,7]{2,1,0:T(8,128)S(1)}, s32[]{:T(128)}, /*index=5*/f32[]{:T(128)}) while((s32[]{:T(128)}, f32[4,8,16,128]{3,2,1,0:T(8,128)}, f32[4,8,16,134]{3,2,1,0:T(8,128)S(1)}, f32[4,8,7]{2,1,0:T(8,128)S(1)}, s32[]{:T(128)}, ...), condition=%wide.region_10.11_spmd, body=%wide.region_9.10_spmd.sunk | while | flops 26345472 | bytes 5110381 | solution.py:40
  74.1 83.2 %all-gather.5.cloned.1.call-done = bf16[64,32,512]{2,1,0:T(8,128)(2,1)} async-done(((bf16[1,32,512]{2,1,0:T(8,128)(2,1)}), bf16[64,32,512]{2,1,0:T(8,128)(2,1)}) %all-gather.5.cloned.1.call-update) | async-done | bytes 2097168 | tf_op jit(solution)/shard_map/all_gather | solution.py:118
  157.3 4.0 fusion.42
  161.3 135.9 %all-gather.3.cloned.1.call-done = bf16[64,32,512]{2,1,0:T(8,128)(2,1)} async-done(((bf16[1,32,512]{2,1,0:T(8,128)(2,1)}), bf16[64,32,512]{2,1,0:T(8,128)(2,1)}) %all-gather.3.cloned.1.call-update) | async-done | bytes 2097168 | tf_op jit(solution)/shard_map/all_gather | solution.py:117
  297.3 4.0 fusion.45
  301.3 20.7 %all-reduce.7 = (bf16[128,32]{0,1:T(8,128)(2,1)S(1)}, bf16[128,32]{0,1:T(8,128)(2,1)S(1)}) all-reduce(f32[128,32]{0,1:T(8,128)S(1)} %fusion.45, f32[128,32]{0,1:T(8,128)S(1)} %fusion.42), channel_id=1, replica_groups=mesh['seq'=64,'ch'=8] {'ch'}, use_global_device_ids=true, to_apply=%region_2.0 | all-reduce | flops 8192 | bytes 49152 | tf_op jit(solution)/shard_map/psum | solution.py:122
  322.0 4.2 fusion.72
  326.2 2.2 collective-permute-start
  328.7 3.1 fusion.69
  333.9 11.6 %all-to-all-start.3 = ((bf16[64,4,512]{2,1,0:T(4,128)(2,1)}), bf16[64,4,512]{2,1,0:T(4,128)(2,1)}, u32[]{:S(2)}, u32[]{:S(2)}) async-start(bf16[64,4,512]{2,1,0:T(4,128)(2,1)} %reshape.208), calls=%async_computation.3 | async-start | bytes 524288 | tf_op jit(solution)/shard_map/all_to_all | solution.py:191
  346.3 14.3 %while.68 = (s32[]{:T(128)}, f32[4,8,16,128]{3,2,1,0:T(8,128)}, f32[4,8,16,134]{3,2,1,0:T(8,128)S(1)}, f32[4,8,7]{2,1,0:T(8,128)S(1)}, s32[]{:T(128)}, /*index=5*/f32[]{:T(128)}) while((s32[]{:T(128)}, f32[4,8,16,128]{3,2,1,0:T(8,128)}, f32[4,8,16,134]{3,2,1,0:T(8,128)S(1)}, f32[4,8,7]{2,1,0:T(8,128)S(1)}, s32[]{:T(128)}, ...), condition=%wide.region_4.5_spmd, body=%wide.region_3.0_spmd.sunk | while | flops 26345472 | bytes 5110381 | solution.py:40
  364.1 4.0 collective-permute-start.1
  368.2 14.1 %all-to-all-start.2 = ((bf16[64,4,32]{2,1,0:T(4,128)(2,1)}), bf16[64,4,32]{2,1,0:T(4,128)(2,1)S(1)}, u32[]{:S(2)}, u32[]{:S(2)}) async-start(bf16[64,4,32]{2,1,0:T(4,128)(2,1)} %bitcast.49), calls=%async_computation.2 | async-start | bytes 131072 | tf_op jit(solution)/shard_map/all_to_all | solution.py:190
  382.8 14.1 %while.72 = (s32[]{:T(128)}, f32[4,8,7]{2,1,0:T(8,128)}, f32[4,8,16,128]{3,2,1,0:T(8,128)S(1)}, f32[4,8,16,134]{3,2,1,0:T(8,128)S(1)}, s32[]{:T(128)}, /*index=5*/s32[]{:T(128)}, f32[]{:T(128)}) while((s32[]{:T(128)}, f32[4,8,7]{2,1,0:T(8,128)}, f32[4,8,16,128]{3,2,1,0:T(8,128)S(1)}, f32[4,8,16,134]{3,2,1,0:T(8,128)S(1)}, s32[]{:T(128)}, ...), condition=%wide.region_16.17_spmd, body=%wide.region_14.16_spmd.sunk | while | flops 26482636 | bytes 4614565 | solution.py:40
  397.7 15.4 %all-to-all-start = ((bf16[64,4,32]{2,1,0:T(4,128)(2,1)}), bf16[64,4,32]{2,1,0:T(4,128)(2,1)S(1)}, u32[]{:S(2)}, u32[]{:S(2)}) async-start(bf16[64,4,32]{2,1,0:T(4,128)(2,1)} %bitcast.46), calls=%async_computation | async-start | bytes 131072 | tf_op jit(solution)/shard_map/all_to_all | solution.py:192
  413.1 1.8 fusion.78
  414.8 13.2 %all-to-all-done = bf16[64,4,32]{2,1,0:T(4,128)(2,1)S(1)} async-done(((bf16[64,4,32]{2,1,0:T(4,128)(2,1)}), bf16[64,4,32]{2,1,0:T(4,128)(2,1)S(1)}, u32[]{:S(2)}, u32[]{:S(2)}) %all-to-all-start) | async-done | bytes 16416 | tf_op jit(solution)/shard_map/all_to_all | solution.py:192
  428.0 1.8 fusion.76
  431.9 7.9 %while.73 = (s32[]{:T(128)}, f32[4,8,128]{2,1,0:T(8,128)S(1)}, f32[4,8,16,128]{3,2,1,0:T(8,128)S(1)}, f32[4,8,16,255]{3,2,1,0:T(8,128)S(1)}, s32[]{:T(128)}, /*index=5*/s32[]{:T(128)}, f32[]{:T(128)}) while((s32[]{:T(128)}, f32[4,8,128]{2,1,0:T(8,128)S(1)}, f32[4,8,16,128]{3,2,1,0:T(8,128)S(1)}, f32[4,8,16,255]{3,2,1,0:T(8,128)S(1)}, ...), condition=%wide.region_20.21_spmd, body=%wide.region_18.20_spmd.sunk | while | flops 50395136 | bytes 6505573 | solution.py:40
  439.8 275.1 %all-reduce.6 = (f32[32,7]{0,1:T(8,128)S(1)}, f32[32,128]{1,0:T(8,128)S(1)}) all-reduce(f32[32,7]{0,1:T(8,128)S(1)} %copy.96, f32[32,128]{1,0:T(8,128)S(1)} %bitcast_multiply_fusion), channel_id=1, replica_groups=mesh['seq'=64,'ch'=8] {'seq'}, use_global_device_ids=true, to_apply=%region_17.18 | all-reduce | flops 4320 | bytes 34560 | tf_op jit(solution)/shard_map/psum | solution.py:166
  716.1 10.5 %while.69 = (s32[]{:T(128)}, f32[4,8,16,128]{3,2,1,0:T(8,128)S(1)}, f32[4,8,16,255]{3,2,1,0:T(8,128)S(1)}, f32[4,8,128]{2,1,0:T(8,128)S(1)}, s32[]{:T(128)}, /*index=5*/f32[]{:T(128)}) while((s32[]{:T(128)}, f32[4,8,16,128]{3,2,1,0:T(8,128)S(1)}, f32[4,8,16,255]{3,2,1,0:T(8,128)S(1)}, f32[4,8,128]{2,1,0:T(8,128)S(1)}, s32[]{:T(128)}, ...), condition=%wide.region_6.7_spmd, body=%wide.region_5.6_spmd.sunk | while | flops 50135040 | bytes 6509645 | solution.py:40
  (275 shorter events, 101.2 us)
Async XLA Ops:
  7.2 7.0 copy-start
  7.2 28.9 %copy-start.12 = (f32[32]{0:T(128)S(1)}, f32[32]{0:T(128)}, u32[]{:S(2)}) copy-start(f32[32]{0:T(128)} %param.39) | copy-start | bytes 388
  7.2 29.0 %copy-start.3 = (f32[32,128]{1,0:T(8,128)S(1)}, f32[32,128]{1,0:T(8,128)}, u32[]{:S(2)}) copy-start(f32[32,128]{1,0:T(8,128)} %param.38) | copy-start | bytes 49156
  7.2 150.0 %all-gather.5.cloned.1.call-start = ((), (), s32[]{:S(2)}) async-start(), calls=%async_computation.5 | async-start | bytes 2129920 | tf_op jit(solution)/shard_map/all_gather | solution.py:118
  10.0 26.6 %collective-permute-start.2 = (bf16[127,512]{0,1:T(8,128)(2,1)S(1)}, bf16[127,512]{0,1:T(8,128)(2,1)S(1)}, u32[]{:S(2)}, u32[]{:S(2)}) collective-permute-start(bf16[127,512]{0,1:T(8,128)(2,1)S(1)} %bitcast.204), channel_id=1, source_target_pairs={{8,0},{16,8},{24,16},{32,24},{40,32},{48,40},{56,48},{64,56},{72,6... | collective-permute-start | bytes 390152 | tf_op jit(solution)/shard_map/ppermute | solution.py:11
  13.7 0.5 copy-start.9
  14.2 21.2 %copy-start.7 = (f32[128]{0:T(128)}, f32[128]{0:T(128)S(1)}, u32[]{:S(2)}) copy-start(f32[128]{0:T(128)S(1)} %multiply_add_fusion) | copy-start | bytes 1540
  15.2 318.7 %all-to-all-start.1 = ((bf16[64,4,512]{2,1,0:T(4,128)(2,1)}), bf16[64,4,512]{2,1,0:T(4,128)(2,1)}, u32[]{:S(2)}, u32[]{:S(2)}) async-start(bf16[64,4,512]{2,1,0:T(4,128)(2,1)} %reshape.205), calls=%async_computation.1 | async-start | bytes 524288 | tf_op jit(solution)/shard_map/all_to_all | solution.py:189
  35.4 261.9 %all-gather.3.cloned.1.call-start = ((), (), s32[]{:S(2)}) async-start(), calls=%async_computation.4 | async-start | bytes 2129920 | tf_op jit(solution)/shard_map/all_gather | solution.py:117
  36.1 0.5 copy-start.5
  37.7 10.8 %copy-start.1 = (bf16[128,512]{1,0:T(8,128)(2,1)S(1)}, bf16[128,512]{1,0:T(8,128)(2,1)}, u32[]{:S(2)}) copy-start(bf16[128,512]{1,0:T(8,128)(2,1)} %param.27) | copy-start | bytes 393220
  37.7 13.9 %copy-start.4 = (f32[32,7]{0,1:T(8,128)S(1)}, f32[32,7]{0,1:T(8,128)}, u32[]{:S(2)}) copy-start(f32[32,7]{0,1:T(8,128)} %param.37) | copy-start | bytes 2692
  49.4 5.5 collective-permute-start.3
  56.5 15.6 %copy-start.8 = (f32[128]{0:T(128)S(1)}, f32[128]{0:T(128)}, u32[]{:S(2)}) copy-start(f32[128]{0:T(128)} %copy-done.7) | copy-start | bytes 1540
  70.8 86.4 %copy-start.2 = (bf16[128,512]{1,0:T(8,128)(2,1)S(1)}, bf16[128,512]{1,0:T(8,128)(2,1)}, u32[]{:S(2)}) copy-start(bf16[128,512]{1,0:T(8,128)(2,1)} %param.28) | copy-start | bytes 393220
  161.3 160.7 %copy-start.11 = (bf16[128,512]{1,0:T(8,128)(2,1)S(1)}, bf16[128,512]{1,0:T(8,128)(2,1)}, u32[]{:S(2)}) copy-start(bf16[128,512]{1,0:T(8,128)(2,1)} %param.29) | copy-start | bytes 393220
  322.0 6.6 copy-start.10
  326.2 7.3 collective-permute-start
  333.9 34.3 %all-to-all-start.3 = ((bf16[64,4,512]{2,1,0:T(4,128)(2,1)}), bf16[64,4,512]{2,1,0:T(4,128)(2,1)}, u32[]{:S(2)}, u32[]{:S(2)}) async-start(bf16[64,4,512]{2,1,0:T(4,128)(2,1)} %reshape.208), calls=%async_computation.3 | async-start | bytes 524288 | tf_op jit(solution)/shard_map/all_to_all | solution.py:191
  364.1 65.6 %collective-permute-start.1 = (bf16[127,512]{1,0:T(8,128)(2,1)}, bf16[127,512]{1,0:T(8,128)(2,1)}, u32[]{:S(2)}, u32[]{:S(2)}) collective-permute-start(bf16[127,512]{1,0:T(8,128)(2,1)} %slice.33), channel_id=1, source_target_pairs={{0,8},{8,16},{16,24},{24,32},{32,40},{40,48},{48,56},{56,64},{64,7... | collective-permute-start | bytes 390152 | tf_op jit(solution)/shard_map/ppermute | solution.py:11
  368.2 29.5 %all-to-all-start.2 = ((bf16[64,4,32]{2,1,0:T(4,128)(2,1)}), bf16[64,4,32]{2,1,0:T(4,128)(2,1)S(1)}, u32[]{:S(2)}, u32[]{:S(2)}) async-start(bf16[64,4,32]{2,1,0:T(4,128)(2,1)} %bitcast.49), calls=%async_computation.2 | async-start | bytes 131072 | tf_op jit(solution)/shard_map/all_to_all | solution.py:190
  397.7 30.3 %all-to-all-start = ((bf16[64,4,32]{2,1,0:T(4,128)(2,1)}), bf16[64,4,32]{2,1,0:T(4,128)(2,1)S(1)}, u32[]{:S(2)}, u32[]{:S(2)}) async-start(bf16[64,4,32]{2,1,0:T(4,128)(2,1)} %bitcast.46), calls=%async_computation | async-start | bytes 131072 | tf_op jit(solution)/shard_map/all_to_all | solution.py:192
  431.8 7.9 %copy-start.6 = (f32[32]{0:T(128)S(1)}, f32[32]{0:T(128)}, u32[]{:S(2)}) copy-start(f32[32]{0:T(128)} %copy-done.5) | copy-start | bytes 388
Sparse Core Ops, SparseCore 0:
  11.0 146.2 all-gather.4
  160.2 137.0 all-gather.2
where the time goes:
time: 735 us; the launch traced here: 734 us
  blocking collectives  296 us (40%)
  waiting for transfers between devices  237 us (32%)
  starting transfers between devices  70.3 us (10%)
  local copies, waits for them, and re-layouts  58.2 us (8%)
  matrix products  50 us (7%)
  between operations  14.5 us (2%)
  other arithmetic  7.68 us (1%)
    psum x1, blocking collectives, on_device(): lax.psum((short_tap_grad, medium_tap_grad * decay_envelope), 'seq')  275 us
    all_gather x1, waiting for transfers between devices, on_device(): lax.all_gather(adapter_down_factor, 'seq', axis=0, tiled=True)  136 us
    all_gather x1, waiting for transfers between devices, on_device(): lax.all_gather(adapter_up_factor, 'seq', axis=0, tiled=True)  83.2 us
    dot_general x24, matrix products, one_block(): jnp.einsum('gts,gcs->gct', band, data, precision=lax.Precision.HIGHEST)  28.5 us
    reshape x24, local copies, waits for them, and re-layouts, band_matrix(): return repeated_groups.reshape(groups, out_len, full_len)  25.7 us
    psum x1, blocking collectives, on_device(): lax.psum(select_codes(contract_last(normalized_layer_entry, flat_down), o...  20.7 us
    all_to_all x1, starting transfers between devices, on_device(): lax.all_to_all(packed[0], 'seq', split_axis=0, concat_axis=0, tiled=True)  20.2 us
    all_to_all x1, starting transfers between devices, on_device(): lax.all_to_all(packed[3], 'seq', split_axis=0, concat_axis=0, tiled=True)  15.4 us
  transfers between devices with their start and end apart: 10, of which 4 were waited for; matrix products, arithmetic and copies ran while one was open for 13% of the time, Pallas kernels for 0%

commit v1 on v0

--- a/solution.py
+++ b/solution.py
@@ -115,7 +115,10 @@
     )
     all_down, all_up = (
         lax.all_gather(adapter_down_factor, "seq", axis=0, tiled=True),
-        lax.all_gather(adapter_up_factor, "seq", axis=0, tiled=True),
+        jnp.concatenate(
+            lax.all_to_all(jnp.stack([adapter_up_factor] * lax.axis_size("seq")), "seq", 0, 0),
+            axis=0,
+        ),
     )
     flat_down = all_down.reshape(seq_count * lowdim_breadth, feature_lanes)
     flat_up = all_up.reshape(seq_count * lowdim_breadth, feature_lanes)

time: 735 us -> 639 us (0.87)
  waiting for transfers between devices: 237 us -> 126 us
  starting transfers between devices: 70.3 us -> 83.1 us
    all_gather x1 -> x0, waiting for transfers between devices: 83.2 us -> none  [on_device(): lax.all_gather(adapter_up_factor, 'seq', axis=0, tiled=True)]
    all_gather x1, waiting for transfers between devices: 136 us -> 106 us  [on_device(): lax.all_gather(adapter_down_factor, 'seq', axis=0, tiled=True)]
    all_to_all x0 -> x1, starting transfers between devices: none -> 19.1 us  [on_device(): lax.all_to_all(jnp.stack([adapter_up_factor] * lax.axis_size('seq')), 'se...]
    all_to_all x1, starting transfers between devices: 20.2 us -> 10.2 us  [on_device(): lax.all_to_all(packed[0], 'seq', split_axis=0, concat_axis=0, tiled=True)]
  transfers between devices with their start and end apart: 10 -> 10, of which waited for: 4 -> 4; matrix products, arithmetic and copies ran while one was open for 13% -> 14% of each run, Pallas kernels for 0% -> 0%
where the time goes in v1:
time: 639 us; the launch traced here: 638 us
  blocking collectives  296 us (46%)
  waiting for transfers between devices  126 us (20%)
  starting transfers between devices  83.1 us (13%)
  local copies, waits for them, and re-layouts  60.6 us (9%)
  matrix products  49.9 us (8%)
  between operations  14.6 us (2%)
  other arithmetic  6.51 us (1%)
    psum x1, blocking collectives, on_device(): lax.psum((short_tap_grad, medium_tap_grad * decay_envelope), 'seq')  275 us
    all_gather x1, waiting for transfers between devices, on_device(): lax.all_gather(adapter_down_factor, 'seq', axis=0, tiled=True)  106 us
    dot_general x24, matrix products, one_block(): jnp.einsum('gts,gcs->gct', band, data, precision=lax.Precision.HIGHEST)  31 us
    reshape x24, local copies, waits for them, and re-layouts, band_matrix(): return repeated_groups.reshape(groups, out_len, full_len)  25.7 us
    psum x1, blocking collectives, on_device(): lax.psum(select_codes(contract_last(normalized_layer_entry, flat_down), o...  21.3 us
    all_to_all x1, starting transfers between devices, on_device(): lax.all_to_all(jnp.stack([adapter_up_factor] * lax.axis_size('seq')), 'se...  19.1 us
    all_to_all x1, starting transfers between devices, on_device(): lax.all_to_all(packed[3], 'seq', split_axis=0, concat_axis=0, tiled=True)  14.9 us
    all_to_all x1, starting transfers between devices, on_device(): lax.all_to_all(packed[2], 'seq', split_axis=0, concat_axis=0, tiled=True)  14.7 us
  transfers between devices with their start and end apart: 10, of which 4 were waited for; matrix products, arithmetic and copies ran while one was open for 14% of the time, Pallas kernels for 0%

profile of v1, /device:TPU:2, one launch (start us, length us, event | category | flops | bytes accessed | tf_op | source)
XLA Modules:
  0.0 638.5 jit_solution(3855336073341729385)
XLA Ops:
  7.2 2.4 stack.2
  9.6 19.1 %all-to-all-start = ((bf16[64,1,32,512]{3,2,1,0:T(8,128)(2,1)}), bf16[64,1,32,512]{3,2,1,0:T(8,128)(2,1)}, u32[]{:S(2)}, u32[]{:S(2)}) async-start(bf16[64,1,32,512]{3,2,1,0:T(8,128)(2,1)} %stack.2), calls=%async_computation | async-start | bytes 4194304 | tf_op jit(solution)/shard_map/all_to_all | solution.py:119
  31.9 4.7 collective-permute-done.2
  38.4 12.9 %while.70 = (s32[]{:T(128)}, f32[4,8,16,128]{3,2,1,0:T(8,128)}, f32[4,8,16,255]{3,2,1,0:T(8,128)S(1)}, f32[4,8,128]{2,1,0:T(8,128)S(1)}, s32[]{:T(128)}, /*index=5*/f32[]{:T(128)}) while((s32[]{:T(128)}, f32[4,8,16,128]{3,2,1,0:T(8,128)}, f32[4,8,16,255]{3,2,1,0:T(8,128)S(1)}, f32[4,8,128]{2,1,0:T(8,128)S(1)}, s32[]{:T(128)}, ...), condition=%wide.region_8.9_spmd, body=%wide.region_7.8_spmd.sunk | while | flops 50135040 | bytes 6509645 | solution.py:40
  56.5 2.7 collective-permute-done.3
  60.7 14.3 %while.71 = (s32[]{:T(128)}, f32[4,8,16,128]{3,2,1,0:T(8,128)}, f32[4,8,16,134]{3,2,1,0:T(8,128)S(1)}, f32[4,8,7]{2,1,0:T(8,128)S(1)}, s32[]{:T(128)}, /*index=5*/f32[]{:T(128)}) while((s32[]{:T(128)}, f32[4,8,16,128]{3,2,1,0:T(8,128)}, f32[4,8,16,134]{3,2,1,0:T(8,128)S(1)}, f32[4,8,7]{2,1,0:T(8,128)S(1)}, s32[]{:T(128)}, ...), condition=%wide.region_10.11_spmd, body=%wide.region_9.10_spmd.sunk | while | flops 26345472 | bytes 5110381 | solution.py:40
  78.1 105.7 %all-gather.2.cloned.1.call-done = bf16[64,32,512]{2,1,0:T(8,128)(2,1)} async-done(((bf16[1,32,512]{2,1,0:T(8,128)(2,1)}), bf16[64,32,512]{2,1,0:T(8,128)(2,1)}) %all-gather.2.cloned.1.call-update) | async-done | bytes 2097168 | tf_op jit(solution)/shard_map/all_gather | solution.py:117
  183.8 4.0 fusion.44
  187.8 10.2 %all-to-all-start.2 = ((bf16[64,4,512]{2,1,0:T(4,128)(2,1)}), bf16[64,4,512]{2,1,0:T(4,128)(2,1)S(1)}, u32[]{:S(2)}, u32[]{:S(2)}) async-start(bf16[64,4,512]{2,1,0:T(4,128)(2,1)} %reshape.216), calls=%async_computation.2 | async-start | bytes 524288 | tf_op jit(solution)/shard_map/all_to_all | solution.py:192
  198.1 4.1 fusion.41
  202.1 21.3 %all-reduce.7 = (bf16[128,32]{0,1:T(8,128)(2,1)S(1)}, bf16[128,32]{0,1:T(8,128)(2,1)S(1)}) all-reduce(f32[128,32]{0,1:T(8,128)S(1)} %fusion.44, f32[128,32]{0,1:T(8,128)S(1)} %fusion.41), channel_id=1, replica_groups=mesh['seq'=64,'ch'=8] {'ch'}, use_global_device_ids=true, to_apply=%region_2.0 | all-reduce | flops 8192 | bytes 49152 | tf_op jit(solution)/shard_map/psum | solution.py:125
  224.0 2.3 fusion.57
  226.3 3.3 collective-permute-start
  229.8 3.1 fusion.54
  235.0 14.7 %all-to-all-start.4 = ((bf16[64,4,512]{2,1,0:T(4,128)(2,1)}), bf16[64,4,512]{2,1,0:T(4,128)(2,1)}, u32[]{:S(2)}, u32[]{:S(2)}) async-start(bf16[64,4,512]{2,1,0:T(4,128)(2,1)} %reshape.219), calls=%async_computation.4 | async-start | bytes 524288 | tf_op jit(solution)/shard_map/all_to_all | solution.py:194
  250.4 14.3 %while.68 = (s32[]{:T(128)}, f32[4,8,16,128]{3,2,1,0:T(8,128)}, f32[4,8,16,134]{3,2,1,0:T(8,128)S(1)}, f32[4,8,7]{2,1,0:T(8,128)S(1)}, s32[]{:T(128)}, /*index=5*/f32[]{:T(128)}) while((s32[]{:T(128)}, f32[4,8,16,128]{3,2,1,0:T(8,128)}, f32[4,8,16,134]{3,2,1,0:T(8,128)S(1)}, f32[4,8,7]{2,1,0:T(8,128)S(1)}, s32[]{:T(128)}, ...), condition=%wide.region_4.5_spmd, body=%wide.region_3.0_spmd.sunk | while | flops 26345472 | bytes 5110381 | solution.py:40
  268.3 4.1 collective-permute-start.1
  272.3 14.3 %all-to-all-start.3 = ((bf16[64,4,32]{2,1,0:T(4,128)(2,1)}), bf16[64,4,32]{2,1,0:T(4,128)(2,1)S(1)}, u32[]{:S(2)}, u32[]{:S(2)}) async-start(bf16[64,4,32]{2,1,0:T(4,128)(2,1)} %bitcast.52), calls=%async_computation.3 | async-start | bytes 131072 | tf_op jit(solution)/shard_map/all_to_all | solution.py:193
  287.2 14.1 %while.72 = (s32[]{:T(128)}, f32[4,8,7]{2,1,0:T(8,128)}, f32[4,8,16,128]{3,2,1,0:T(8,128)S(1)}, f32[4,8,16,134]{3,2,1,0:T(8,128)S(1)}, s32[]{:T(128)}, /*index=5*/s32[]{:T(128)}, f32[]{:T(128)}) while((s32[]{:T(128)}, f32[4,8,7]{2,1,0:T(8,128)}, f32[4,8,16,128]{3,2,1,0:T(8,128)S(1)}, f32[4,8,16,134]{3,2,1,0:T(8,128)S(1)}, s32[]{:T(128)}, ...), condition=%wide.region_16.17_spmd, body=%wide.region_14.16_spmd.sunk | while | flops 26482636 | bytes 4614565 | solution.py:40
  302.1 14.9 %all-to-all-start.1 = ((bf16[64,4,32]{2,1,0:T(4,128)(2,1)}), bf16[64,4,32]{2,1,0:T(4,128)(2,1)S(1)}, u32[]{:S(2)}, u32[]{:S(2)}) async-start(bf16[64,4,32]{2,1,0:T(4,128)(2,1)} %bitcast.49), calls=%async_computation.1 | async-start | bytes 131072 | tf_op jit(solution)/shard_map/all_to_all | solution.py:195
  318.7 13.4 %all-to-all-done.1 = bf16[64,4,32]{2,1,0:T(4,128)(2,1)S(1)} async-done(((bf16[64,4,32]{2,1,0:T(4,128)(2,1)}), bf16[64,4,32]{2,1,0:T(4,128)(2,1)S(1)}, u32[]{:S(2)}, u32[]{:S(2)}) %all-to-all-start.1) | async-done | bytes 16416 | tf_op jit(solution)/shard_map/all_to_all | solution.py:195
  336.0 7.9 %while.73 = (s32[]{:T(128)}, f32[4,8,128]{2,1,0:T(8,128)S(1)}, f32[4,8,16,128]{3,2,1,0:T(8,128)S(1)}, f32[4,8,16,255]{3,2,1,0:T(8,128)S(1)}, s32[]{:T(128)}, /*index=5*/s32[]{:T(128)}, f32[]{:T(128)}) while((s32[]{:T(128)}, f32[4,8,128]{2,1,0:T(8,128)S(1)}, f32[4,8,16,128]{3,2,1,0:T(8,128)S(1)}, f32[4,8,16,255]{3,2,1,0:T(8,128)S(1)}, ...), condition=%wide.region_20.21_spmd, body=%wide.region_18.20_spmd.sunk | while | flops 50395136 | bytes 6505573 | solution.py:40
  344.0 275.1 %all-reduce.6 = (f32[32,7]{0,1:T(8,128)S(1)}, f32[32,128]{1,0:T(8,128)S(1)}) all-reduce(f32[32,7]{0,1:T(8,128)S(1)} %copy.96, f32[32,128]{1,0:T(8,128)S(1)} %bitcast_multiply_fusion), channel_id=1, replica_groups=mesh['seq'=64,'ch'=8] {'seq'}, use_global_device_ids=true, to_apply=%region_17.18 | all-reduce | flops 4320 | bytes 34560 | tf_op jit(solution)/shard_map/psum | solution.py:169
  620.3 10.5 %while.69 = (s32[]{:T(128)}, f32[4,8,16,128]{3,2,1,0:T(8,128)S(1)}, f32[4,8,16,255]{3,2,1,0:T(8,128)S(1)}, f32[4,8,128]{2,1,0:T(8,128)S(1)}, s32[]{:T(128)}, /*index=5*/f32[]{:T(128)}) while((s32[]{:T(128)}, f32[4,8,16,128]{3,2,1,0:T(8,128)S(1)}, f32[4,8,16,255]{3,2,1,0:T(8,128)S(1)}, f32[4,8,128]{2,1,0:T(8,128)S(1)}, s32[]{:T(128)}, ...), condition=%wide.region_6.7_spmd, body=%wide.region_5.6_spmd.sunk | while | flops 50135040 | bytes 6509645 | solution.py:40
  (287 shorter events, 103.8 us)
Async XLA Ops:
  7.2 23.6 %copy-start = (bf16[128,512]{1,0:T(8,128)(2,1)S(1)}, bf16[128,512]{1,0:T(8,128)(2,1)}, u32[]{:S(2)}) copy-start(bf16[128,512]{1,0:T(8,128)(2,1)} %param.26) | copy-start | bytes 393220
  9.6 19.2 %copy-start.5 = (bf16[128,512]{1,0:T(8,128)(2,1)S(1)}, bf16[128,512]{1,0:T(8,128)(2,1)}, u32[]{:S(2)}) copy-start(bf16[128,512]{1,0:T(8,128)(2,1)} %param.30) | copy-start | bytes 393220
  9.6 19.4 %copy-start.6 = (bf16[128,512]{1,0:T(8,128)(2,1)S(1)}, bf16[128,512]{1,0:T(8,128)(2,1)}, u32[]{:S(2)}) copy-start(bf16[128,512]{1,0:T(8,128)(2,1)} %param.32) | copy-start | bytes 393220
  9.6 20.9 %copy-start.15 = (s32[64]{0:T(128)S(1)}, s32[64]{0:T(128)}, u32[]{:S(2)}) copy-start(s32[64]{0:T(128)} %param.36) | copy-start | bytes 772
  9.6 20.9 %copy-start.16 = (s32[128,1]{0,1:T(1,128)S(1)}, s32[128,1]{0,1:T(1,128)}, u32[]{:S(2)}) copy-start(s32[128,1]{0,1:T(1,128)} %param.35) | copy-start | bytes 1540
  9.6 21.7 %copy-start.17 = (f32[32]{0:T(128)S(1)}, f32[32]{0:T(128)}, u32[]{:S(2)}) copy-start(f32[32]{0:T(128)} %param.39) | copy-start | bytes 388
  9.6 21.7 %copy-start.7 = (f32[32,128]{1,0:T(8,128)S(1)}, f32[32,128]{1,0:T(8,128)}, u32[]{:S(2)}) copy-start(f32[32,128]{1,0:T(8,128)} %param.38) | copy-start | bytes 49156
  9.6 178.2 %all-to-all-start = ((bf16[64,1,32,512]{3,2,1,0:T(8,128)(2,1)}), bf16[64,1,32,512]{3,2,1,0:T(8,128)(2,1)}, u32[]{:S(2)}, u32[]{:S(2)}) async-start(bf16[64,1,32,512]{3,2,1,0:T(8,128)(2,1)} %stack.2), calls=%async_computation | async-start | bytes 4194304 | tf_op jit(solution)/shard_map/all_to_all | solution.py:119
  28.8 155.0 %all-gather.2.cloned.1.call-start = ((), (), s32[]{:S(2)}) async-start(), calls=%async_computation.5 | async-start | bytes 2129920 | tf_op jit(solution)/shard_map/all_gather | solution.py:117
  29.1 7.5 %collective-permute-start.2 = (bf16[127,512]{0,1:T(8,128)(2,1)S(1)}, bf16[127,512]{0,1:T(8,128)(2,1)S(1)}, u32[]{:S(2)}, u32[]{:S(2)}) collective-permute-start(bf16[127,512]{0,1:T(8,128)(2,1)S(1)} %bitcast.203), channel_id=1, source_target_pairs={{8,0},{16,8},{24,16},{32,24},{40,32},{48,40},{56,48},{64,56},{72,6... | collective-permute-start | bytes 390152 | tf_op jit(solution)/shard_map/ppermute | solution.py:11
  38.4 14.1 %copy-start.2 = (bf16[128,512]{1,0:T(8,128)(2,1)S(1)}, bf16[128,512]{1,0:T(8,128)(2,1)}, u32[]{:S(2)}) copy-start(bf16[128,512]{1,0:T(8,128)(2,1)} %param.27) | copy-start | bytes 393220
  38.4 17.1 %copy-start.8 = (f32[32,7]{0,1:T(8,128)S(1)}, f32[32,7]{0,1:T(8,128)}, u32[]{:S(2)}) copy-start(f32[32,7]{0,1:T(8,128)} %param.37) | copy-start | bytes 2692
  53.5 5.6 collective-permute-start.3
  60.7 15.5 %copy-start.12 = (f32[128]{0:T(128)S(1)}, f32[128]{0:T(128)}, u32[]{:S(2)}) copy-start(f32[128]{0:T(128)} %copy-done.11) | copy-start | bytes 1540
  77.4 120.7 %copy-start.3 = (bf16[128,512]{1,0:T(8,128)(2,1)S(1)}, bf16[128,512]{1,0:T(8,128)(2,1)}, u32[]{:S(2)}) copy-start(bf16[128,512]{1,0:T(8,128)(2,1)} %param.28) | copy-start | bytes 393220
  187.8 47.2 %all-to-all-start.2 = ((bf16[64,4,512]{2,1,0:T(4,128)(2,1)}), bf16[64,4,512]{2,1,0:T(4,128)(2,1)S(1)}, u32[]{:S(2)}, u32[]{:S(2)}) async-start(bf16[64,4,512]{2,1,0:T(4,128)(2,1)} %reshape.216), calls=%async_computation.2 | async-start | bytes 524288 | tf_op jit(solution)/shard_map/all_to_all | solution.py:192
  198.0 25.9 %copy-start.4 = (bf16[128,512]{1,0:T(8,128)(2,1)S(1)}, bf16[128,512]{1,0:T(8,128)(2,1)}, u32[]{:S(2)}) copy-start(bf16[128,512]{1,0:T(8,128)(2,1)} %param.29) | copy-start | bytes 393220
  226.3 8.4 %collective-permute-start = (bf16[6,512]{1,0:T(8,128)(2,1)S(1)}, bf16[6,512]{1,0:T(8,128)(2,1)S(1)}, u32[]{:S(2)}, u32[]{:S(2)}) collective-permute-start(bf16[6,512]{1,0:T(8,128)(2,1)S(1)} %slice.32), channel_id=1, source_target_pairs={{0,8},{8,16},{16,24},{24,32},{32,40},{40,48},{48,56},{56,64},{64,7... | collective-permute-start | bytes 18440 | tf_op jit(solution)/shard_map/ppermute | solution.py:11
  235.0 15.4 %copy-start.1 = (bf16[64,4,512]{2,1,0:T(4,128)(2,1)}, bf16[64,4,512]{2,1,0:T(4,128)(2,1)S(1)}, u32[]{:S(2)}) copy-start(bf16[64,4,512]{2,1,0:T(4,128)(2,1)S(1)} %all-to-all-done.2) | copy-start | bytes 786436
  235.0 37.3 %all-to-all-start.4 = ((bf16[64,4,512]{2,1,0:T(4,128)(2,1)}), bf16[64,4,512]{2,1,0:T(4,128)(2,1)}, u32[]{:S(2)}, u32[]{:S(2)}) async-start(bf16[64,4,512]{2,1,0:T(4,128)(2,1)} %reshape.219), calls=%async_computation.4 | async-start | bytes 524288 | tf_op jit(solution)/shard_map/all_to_all | solution.py:194
  268.3 65.6 %collective-permute-start.1 = (bf16[127,512]{1,0:T(8,128)(2,1)}, bf16[127,512]{1,0:T(8,128)(2,1)}, u32[]{:S(2)}, u32[]{:S(2)}) collective-permute-start(bf16[127,512]{1,0:T(8,128)(2,1)} %slice.33), channel_id=1, source_target_pairs={{0,8},{8,16},{16,24},{24,32},{32,40},{40,48},{48,56},{56,64},{64,7... | collective-permute-start | bytes 390152 | tf_op jit(solution)/shard_map/ppermute | solution.py:11
  272.3 29.8 %all-to-all-start.3 = ((bf16[64,4,32]{2,1,0:T(4,128)(2,1)}), bf16[64,4,32]{2,1,0:T(4,128)(2,1)S(1)}, u32[]{:S(2)}, u32[]{:S(2)}) async-start(bf16[64,4,32]{2,1,0:T(4,128)(2,1)} %bitcast.52), calls=%async_computation.3 | async-start | bytes 131072 | tf_op jit(solution)/shard_map/all_to_all | solution.py:193
  302.1 30.1 %all-to-all-start.1 = ((bf16[64,4,32]{2,1,0:T(4,128)(2,1)}), bf16[64,4,32]{2,1,0:T(4,128)(2,1)S(1)}, u32[]{:S(2)}, u32[]{:S(2)}) async-start(bf16[64,4,32]{2,1,0:T(4,128)(2,1)} %bitcast.49), calls=%async_computation.1 | async-start | bytes 131072 | tf_op jit(solution)/shard_map/all_to_all | solution.py:195
  336.0 7.9 %copy-start.10 = (f32[32]{0:T(128)S(1)}, f32[32]{0:T(128)}, u32[]{:S(2)}) copy-start(f32[32]{0:T(128)} %copy-done.9) | copy-start | bytes 388
  (4 other events, 7.8 us)
Sparse Core Ops, SparseCore 0:
  32.5 151.2 all-gather.1
